TPU v7x, 32 devices: a whole 2x2x4 slice. The times are simulated.
32 devices in a mesh: mesh: 8 (over y, x, core), band: 4 (over z).
Axes of the slice: x: 2, y: 2, z: 4, core: 2. Of those that a mesh axis runs over, the one named last changes fastest.
Arguments:
- states: float32 [2, 64, 8192], P(None, 'band', 'mesh'), may hold values from -6 to 6
- frozen: float32 [2, 32, 8192], P(None, 'band', 'mesh'), may hold values from -0.125 to 0.125
- weights: float32 [8, 8192], P(None, 'mesh'), may hold values from 0.1 to 1
- potential: float32 [8192], P('mesh'), may hold values from -2 to 2
- send_list: int32 [8, 8, 256], P('mesh'), may hold values from 0 to 1023
- neighbours: int32 [8, 8192], P(None, 'mesh'), may hold values from 0 to 3071, as said below
Outputs:
- evolved: float32 [2, 64, 8192], P(None, 'band', 'mesh')
Inputs may be any that keep to these rules, and one draw needn't show every extreme that they name: `neighbours`: an entry below 1024 names a point of the same part; an entry 1024 + s * 256 + c names ghost slot c from part s, where part s is at most 3 parts away in the cyclic order of parts or exactly half the number of parts away, and every part names ghost slots from all those parts. Slots of send_list[s, i] that part i never names hold arbitrary points of part s.
All inputs are finite; a program needn't handle non-finite values.
Results may differ from a plain program's by a relative error of at most 0.0001.
Values sent between devices are 32-bit elements; how exact they have to be, the bound alone decides.
No kernel may reach another device: no remote copies, remote signals or barrier semaphores. Data moves between devices by JAX's collectives and lax.ppermute only.
A program may use at most 128 MiB of HBM per device.

v0:
```python
import jax
import jax.numpy as jnp
from jax import lax
from jax.sharding import PartitionSpec as P

NBRS = 8
TERMS = 4
time_step = 0.3


def rotate(field):
    return jnp.stack([field[1], -field[0]])


def body(states, frozen, weights, potential, send_list, neighbours):
    parts = lax.axis_size("mesh")
    rows = states.shape[1]
    capacity = send_list.shape[2]
    routes = send_list[0]
    full_frozen = lax.all_gather(frozen, "band", axis=1, tiled=True)
    total = states
    term = states
    for order in range(1, TERMS + 1):
        paired = jnp.stack([term, rotate(term)])
        partial_intersection = jnp.einsum(
            "cmp,ocjp->omj", full_frozen, paired, precision=lax.Precision.HIGHEST
        )
        intersection = lax.psum(partial_intersection, "mesh")
        packed = jnp.take(term, routes.reshape(-1), axis=2).reshape(2, rows, parts, capacity)
        arrived = lax.all_to_all(packed, "mesh", split_axis=2, concat_axis=2, tiled=True)
        extended = jnp.concatenate([term, arrived.reshape(2, rows, parts * capacity)], axis=2)
        stencil = jnp.zeros_like(term)
        for apply_order in range(NBRS):
            stencil = stencil + weights[apply_order] * (
                jnp.take(extended, neighbours[apply_order], axis=2) - term
            )
        blocks = jnp.stack(
            [
                jnp.stack([intersection[0], -intersection[1]]),
                jnp.stack([intersection[1], intersection[0]]),
            ]
        )
        exchange = jnp.einsum("dmp,cdmj->cjp", full_frozen, blocks, precision=lax.Precision.HIGHEST)
        image = -0.5 * stencil + potential * term - exchange
        term = time_step / order * rotate(image)
        total = total + term
    return total


def solution(mesh):
    return jax.shard_map(
        body,
        mesh=mesh,
        in_specs=(
            P(None, "band", "mesh"),
            P(None, "band", "mesh"),
            P(None, "mesh"),
            P("mesh"),
            P("mesh", None, None),
            P(None, "mesh"),
        ),
        out_specs=P(None, "band", "mesh"),
        check_vma=False,
    )
```

profile of v0, /device:TPU:0, one launch (start us, length us, event | category | flops | bytes accessed | tf_op | source)
XLA Modules:
  0.0 581.9 jit_solution(13586005560089532101)
XLA Ops:
  2.1 14.4 %gather_fusion = f32[2048,2,16]{2,1,0:T(2,128)} fusion(f32[2,16,1024]{1,0,2:T(2,128)S(1)} %copy.119, s32[2048]{0:T(1024)S(1)} %fusion.108), kind=kCustom, calls=%fused_computation.clone | custom fusion | bytes 532480 | tf_op jit(solution)/shard_map/jit(_take)/gather | solution.py:29
  16.5 10.0 %broadcast_select_fusion.3 = f32[2048,2,16]{2,1,0:T(2,128)S(1)} fusion(f32[2048,2,16]{2,1,0:T(2,128)} %gather_fusion, pred[2048]{0:T(1024)(128)(4,1)S(1)} %compare_and_fusion), kind=kLoop, calls=%fused_computation.39 | loop fusion | flops 65536 | bytes 526336 | tf_op jit(solution)/shard_map/jit(_take)/select_n | solution.py:29
  39.6 14.2 %all_gather.3 = f32[2,32,1024]{2,1,0:T(8,128)S(1)} all-gather(f32[2,8,1024]{2,1,0:T(8,128)S(1)} %copy-done.34), channel_id=1, replica_groups=mesh['mesh'=8,'band'=4] {'band'}, dimensions={1}, use_global_device_ids=true | all-gather | bytes 327680 | tf_op jit(solution)/shard_map/all_gather | solution.py:20
  54.3 23.0 %psum.28 = f32[2,32,16]{1,2,0:T(8,128)S(1)} all-reduce(f32[2,32,16]{1,2,0:T(8,128)S(1)} %convolution_bitcast_fusion.7), channel_id=1, replica_groups=mesh['mesh'=8,'band'=4] {'mesh'}, use_global_device_ids=true, to_apply=%region_0.3 | all-reduce | flops 1024 | bytes 8192 | tf_op jit(solution)/shard_map/psum | solution.py:28
  84.0 7.6 %gather_fusion.1 = f32[1024,2,16]{2,1,0:T(2,128)} fusion(f32[2,16,3072]{1,0,2:T(2,128)S(1)} %copy.122, s32[1024]{0:T(1024)} %fusion.109), kind=kCustom, calls=%fused_computation.1.clone | custom fusion | bytes 266240 | tf_op jit(solution)/shard_map/jit(_take)/gather | solution.py:35
  93.7 7.6 %gather_fusion.2 = f32[1024,2,16]{2,1,0:T(2,128)} fusion(f32[2,16,3072]{1,0,2:T(2,128)S(1)} %copy.122, s32[1024]{0:T(1024)} %fusion.110), kind=kCustom, calls=%fused_computation.5.clone | custom fusion | bytes 266240 | tf_op jit(solution)/shard_map/jit(_take)/gather | solution.py:35
  103.3 7.6 %gather_fusion.3 = f32[1024,2,16]{2,1,0:T(2,128)} fusion(f32[2,16,3072]{1,0,2:T(2,128)S(1)} %copy.122, s32[1024]{0:T(1024)} %fusion.111), kind=kCustom, calls=%fused_computation.6.clone | custom fusion | bytes 266240 | tf_op jit(solution)/shard_map/jit(_take)/gather | solution.py:35
  112.9 7.6 %gather_fusion.4 = f32[1024,2,16]{2,1,0:T(2,128)} fusion(f32[2,16,3072]{1,0,2:T(2,128)S(1)} %copy.122, s32[1024]{0:T(1024)} %fusion.112), kind=kCustom, calls=%fused_computation.7.clone | custom fusion | bytes 266240 | tf_op jit(solution)/shard_map/jit(_take)/gather | solution.py:35
  122.5 7.6 %gather_fusion.5 = f32[1024,2,16]{2,1,0:T(2,128)} fusion(f32[2,16,3072]{1,0,2:T(2,128)S(1)} %copy.122, s32[1024]{0:T(1024)} %fusion.113), kind=kCustom, calls=%fused_computation.8.clone | custom fusion | bytes 266240 | tf_op jit(solution)/shard_map/jit(_take)/gather | solution.py:35
  132.1 7.6 %gather_fusion.6 = f32[1024,2,16]{2,1,0:T(2,128)} fusion(f32[2,16,3072]{1,0,2:T(2,128)S(1)} %copy.122, s32[1024]{0:T(1024)} %fusion.114), kind=kCustom, calls=%fused_computation.9.clone | custom fusion | bytes 266240 | tf_op jit(solution)/shard_map/jit(_take)/gather | solution.py:35
  141.7 7.5 %gather_fusion.7 = f32[1024,2,16]{2,1,0:T(2,128)} fusion(f32[2,16,3072]{1,0,2:T(2,128)S(1)} %copy.122, s32[1024]{0:T(1024)S(1)} %fusion.115), kind=kCustom, calls=%fused_computation.10.clone | custom fusion | bytes 266240 | tf_op jit(solution)/shard_map/jit(_take)/gather | solution.py:35
  151.2 7.5 %gather_fusion.8 = f32[1024,2,16]{2,1,0:T(2,128)} fusion(f32[2,16,3072]{1,0,2:T(2,128)S(1)} %copy.122, s32[1024]{0:T(1024)S(1)} %fusion.116), kind=kCustom, calls=%fused_computation.11.clone | custom fusion | bytes 266240 | tf_op jit(solution)/shard_map/jit(_take)/gather | solution.py:35
  163.5 22.3 %psum.29 = f32[2,32,16]{1,2,0:T(8,128)S(1)} all-reduce(f32[2,32,16]{1,2,0:T(8,128)S(1)} %convolution_bitcast_fusion.6), channel_id=1, replica_groups=mesh['mesh'=8,'band'=4] {'mesh'}, use_global_device_ids=true, to_apply=%region_1.4 | all-reduce | flops 1024 | bytes 8192 | tf_op jit(solution)/shard_map/psum | solution.py:28
  185.8 14.4 %gather_fusion.9 = f32[2048,2,16]{2,1,0:T(2,128)} fusion(f32[2,16,1024]{1,0,2:T(2,128)S(1)} %copy.138, s32[2048]{0:T(1024)S(1)} %fusion.108), kind=kCustom, calls=%fused_computation.2.clone | custom fusion | bytes 532480 | tf_op jit(solution)/shard_map/jit(_take)/gather | solution.py:29
  200.2 10.0 %broadcast_select_fusion.2 = f32[2048,2,16]{2,1,0:T(2,128)S(1)} fusion(f32[2048,2,16]{2,1,0:T(2,128)} %gather_fusion.9, pred[2048]{0:T(1024)(128)(4,1)S(1)} %copy-done.36), kind=kLoop, calls=%fused_computation.38 | loop fusion | flops 65536 | bytes 526336 | tf_op jit(solution)/shard_map/jit(_take)/select_n | solution.py:29
  216.3 6.1 %all-to-all-done.1 = f32[2,16,8,256]{3,1,0,2:T(8,128)S(1)} async-done(((f32[2,16,8,256]{3,1,0,2:T(8,128)}), f32[2,16,8,256]{3,1,0,2:T(8,128)S(1)}, u32[]{:S(2)}, u32[]{:S(2)}) %all-to-all-start.1) | async-done | bytes 262176 | tf_op jit(solution)/shard_map/all_to_all | solution.py:30
  227.3 7.6 %gather_fusion.10 = f32[1024,2,16]{2,1,0:T(2,128)} fusion(f32[2,16,3072]{1,0,2:T(2,128)S(1)} %copy.141, s32[1024]{0:T(1024)} %fusion.109), kind=kCustom, calls=%fused_computation.12.clone | custom fusion | bytes 266240 | tf_op jit(solution)/shard_map/jit(_take)/gather | solution.py:35
  235.0 7.6 %gather_fusion.11 = f32[1024,2,16]{2,1,0:T(2,128)} fusion(f32[2,16,3072]{1,0,2:T(2,128)S(1)} %copy.141, s32[1024]{0:T(1024)} %fusion.110), kind=kCustom, calls=%fused_computation.13.clone | custom fusion | bytes 266240 | tf_op jit(solution)/shard_map/jit(_take)/gather | solution.py:35
  242.6 7.6 %gather_fusion.12 = f32[1024,2,16]{2,1,0:T(2,128)} fusion(f32[2,16,3072]{1,0,2:T(2,128)S(1)} %copy.141, s32[1024]{0:T(1024)} %fusion.111), kind=kCustom, calls=%fused_computation.14.clone | custom fusion | bytes 266240 | tf_op jit(solution)/shard_map/jit(_take)/gather | solution.py:35
  250.2 7.6 %gather_fusion.13 = f32[1024,2,16]{2,1,0:T(2,128)} fusion(f32[2,16,3072]{1,0,2:T(2,128)S(1)} %copy.141, s32[1024]{0:T(1024)} %fusion.112), kind=kCustom, calls=%fused_computation.15.clone | custom fusion | bytes 266240 | tf_op jit(solution)/shard_map/jit(_take)/gather | solution.py:35
  257.8 7.6 %gather_fusion.14 = f32[1024,2,16]{2,1,0:T(2,128)} fusion(f32[2,16,3072]{1,0,2:T(2,128)S(1)} %copy.141, s32[1024]{0:T(1024)} %fusion.113), kind=kCustom, calls=%fused_computation.16.clone | custom fusion | bytes 266240 | tf_op jit(solution)/shard_map/jit(_take)/gather | solution.py:35
  265.4 7.6 %gather_fusion.15 = f32[1024,2,16]{2,1,0:T(2,128)} fusion(f32[2,16,3072]{1,0,2:T(2,128)S(1)} %copy.141, s32[1024]{0:T(1024)} %fusion.114), kind=kCustom, calls=%fused_computation.17.clone | custom fusion | bytes 266240 | tf_op jit(solution)/shard_map/jit(_take)/gather | solution.py:35
  273.0 7.5 %gather_fusion.16 = f32[1024,2,16]{2,1,0:T(2,128)} fusion(f32[2,16,3072]{1,0,2:T(2,128)S(1)} %copy.141, s32[1024]{0:T(1024)S(1)} %fusion.115), kind=kCustom, calls=%fused_computation.18.clone | custom fusion | bytes 266240 | tf_op jit(solution)/shard_map/jit(_take)/gather | solution.py:35
  280.5 7.5 %gather_fusion.17 = f32[1024,2,16]{2,1,0:T(2,128)} fusion(f32[2,16,3072]{1,0,2:T(2,128)S(1)} %copy.141, s32[1024]{0:T(1024)S(1)} %fusion.116), kind=kCustom, calls=%fused_computation.19.clone | custom fusion | bytes 266240 | tf_op jit(solution)/shard_map/jit(_take)/gather | solution.py:35
  303.7 22.3 %psum.30 = f32[2,32,16]{1,2,0:T(8,128)S(1)} all-reduce(f32[2,32,16]{1,2,0:T(8,128)S(1)} %convolution_bitcast_fusion.5), channel_id=1, replica_groups=mesh['mesh'=8,'band'=4] {'mesh'}, use_global_device_ids=true, to_apply=%region_2.5 | all-reduce | flops 1024 | bytes 8192 | tf_op jit(solution)/shard_map/psum | solution.py:28
  326.0 14.4 %gather_fusion.18 = f32[2048,2,16]{2,1,0:T(2,128)} fusion(f32[2,16,1024]{1,0,2:T(2,128)S(1)} %copy.157, s32[2048]{0:T(1024)S(1)} %fusion.108), kind=kCustom, calls=%fused_computation.3.clone | custom fusion | bytes 532480 | tf_op jit(solution)/shard_map/jit(_take)/gather | solution.py:29
  340.4 10.0 %broadcast_select_fusion.1 = f32[2048,2,16]{2,1,0:T(2,128)S(1)} fusion(f32[2048,2,16]{2,1,0:T(2,128)} %gather_fusion.18, pred[2048]{0:T(1024)(128)(4,1)S(1)} %copy-done.37), kind=kLoop, calls=%fused_computation.37 | loop fusion | flops 65536 | bytes 526336 | tf_op jit(solution)/shard_map/jit(_take)/select_n | solution.py:29
  356.3 6.2 %all-to-all-done.2 = f32[2,16,8,256]{3,1,0,2:T(8,128)S(1)} async-done(((f32[2,16,8,256]{3,1,0,2:T(8,128)}), f32[2,16,8,256]{3,1,0,2:T(8,128)S(1)}, u32[]{:S(2)}, u32[]{:S(2)}) %all-to-all-start.2) | async-done | bytes 262176 | tf_op jit(solution)/shard_map/all_to_all | solution.py:30
  367.5 7.6 %gather_fusion.19 = f32[1024,2,16]{2,1,0:T(2,128)} fusion(f32[2,16,3072]{1,0,2:T(2,128)S(1)} %copy.160, s32[1024]{0:T(1024)} %fusion.109), kind=kCustom, calls=%fused_computation.20.clone | custom fusion | bytes 266240 | tf_op jit(solution)/shard_map/jit(_take)/gather | solution.py:35
  375.2 7.6 %gather_fusion.20 = f32[1024,2,16]{2,1,0:T(2,128)} fusion(f32[2,16,3072]{1,0,2:T(2,128)S(1)} %copy.160, s32[1024]{0:T(1024)} %fusion.110), kind=kCustom, calls=%fused_computation.21.clone | custom fusion | bytes 266240 | tf_op jit(solution)/shard_map/jit(_take)/gather | solution.py:35
  382.8 7.6 %gather_fusion.21 = f32[1024,2,16]{2,1,0:T(2,128)} fusion(f32[2,16,3072]{1,0,2:T(2,128)S(1)} %copy.160, s32[1024]{0:T(1024)} %fusion.111), kind=kCustom, calls=%fused_computation.22.clone | custom fusion | bytes 266240 | tf_op jit(solution)/shard_map/jit(_take)/gather | solution.py:35
  390.4 7.6 %gather_fusion.22 = f32[1024,2,16]{2,1,0:T(2,128)} fusion(f32[2,16,3072]{1,0,2:T(2,128)S(1)} %copy.160, s32[1024]{0:T(1024)} %fusion.112), kind=kCustom, calls=%fused_computation.23.clone | custom fusion | bytes 266240 | tf_op jit(solution)/shard_map/jit(_take)/gather | solution.py:35
  398.0 7.6 %gather_fusion.23 = f32[1024,2,16]{2,1,0:T(2,128)} fusion(f32[2,16,3072]{1,0,2:T(2,128)S(1)} %copy.160, s32[1024]{0:T(1024)} %fusion.113), kind=kCustom, calls=%fused_computation.24.clone | custom fusion | bytes 266240 | tf_op jit(solution)/shard_map/jit(_take)/gather | solution.py:35
  405.6 7.6 %gather_fusion.24 = f32[1024,2,16]{2,1,0:T(2,128)} fusion(f32[2,16,3072]{1,0,2:T(2,128)S(1)} %copy.160, s32[1024]{0:T(1024)} %fusion.114), kind=kCustom, calls=%fused_computation.25.clone | custom fusion | bytes 266240 | tf_op jit(solution)/shard_map/jit(_take)/gather | solution.py:35
  413.2 7.5 %gather_fusion.25 = f32[1024,2,16]{2,1,0:T(2,128)} fusion(f32[2,16,3072]{1,0,2:T(2,128)S(1)} %copy.160, s32[1024]{0:T(1024)S(1)} %fusion.115), kind=kCustom, calls=%fused_computation.26.clone | custom fusion | bytes 266240 | tf_op jit(solution)/shard_map/jit(_take)/gather | solution.py:35
  420.7 7.5 %gather_fusion.26 = f32[1024,2,16]{2,1,0:T(2,128)} fusion(f32[2,16,3072]{1,0,2:T(2,128)S(1)} %copy.160, s32[1024]{0:T(1024)S(1)} %fusion.116), kind=kCustom, calls=%fused_computation.27.clone | custom fusion | bytes 266240 | tf_op jit(solution)/shard_map/jit(_take)/gather | solution.py:35
  443.8 22.3 %psum.31 = f32[2,32,16]{1,2,0:T(8,128)S(1)} all-reduce(f32[2,32,16]{1,2,0:T(8,128)S(1)} %convolution_bitcast_fusion.4), channel_id=1, replica_groups=mesh['mesh'=8,'band'=4] {'mesh'}, use_global_device_ids=true, to_apply=%region_3.6 | all-reduce | flops 1024 | bytes 8192 | tf_op jit(solution)/shard_map/psum | solution.py:28
  466.1 14.4 %gather_fusion.27 = f32[2048,2,16]{2,1,0:T(2,128)} fusion(f32[2,16,1024]{1,0,2:T(2,128)S(1)} %copy.176, s32[2048]{0:T(1024)S(1)} %fusion.108), kind=kCustom, calls=%fused_computation.4.clone | custom fusion | bytes 532480 | tf_op jit(solution)/shard_map/jit(_take)/gather | solution.py:29
  480.6 10.0 %broadcast_select_fusion = f32[2048,2,16]{2,1,0:T(2,128)S(1)} fusion(f32[2048,2,16]{2,1,0:T(2,128)} %gather_fusion.27, pred[2048]{0:T(1024)(128)(4,1)S(1)} %copy-done.38), kind=kLoop, calls=%fused_computation.36 | loop fusion | flops 65536 | bytes 526336 | tf_op jit(solution)/shard_map/jit(_take)/select_n | solution.py:29
  496.8 6.0 %all-to-all-done.3 = f32[2,16,8,256]{3,1,0,2:T(8,128)S(1)} async-done(((f32[2,16,8,256]{3,1,0,2:T(8,128)}), f32[2,16,8,256]{3,1,0,2:T(8,128)S(1)}, u32[]{:S(2)}, u32[]{:S(2)}) %all-to-all-start.3) | async-done | bytes 262176 | tf_op jit(solution)/shard_map/all_to_all | solution.py:30
  507.8 7.6 %gather_fusion.28 = f32[1024,2,16]{2,1,0:T(2,128)} fusion(f32[2,16,3072]{1,0,2:T(2,128)S(1)} %copy.179, s32[1024]{0:T(1024)} %fusion.109), kind=kCustom, calls=%fused_computation.28.clone | custom fusion | bytes 266240 | tf_op jit(solution)/shard_map/jit(_take)/gather | solution.py:35
  515.4 7.6 %gather_fusion.29 = f32[1024,2,16]{2,1,0:T(2,128)} fusion(f32[2,16,3072]{1,0,2:T(2,128)S(1)} %copy.179, s32[1024]{0:T(1024)} %fusion.110), kind=kCustom, calls=%fused_computation.29.clone | custom fusion | bytes 266240 | tf_op jit(solution)/shard_map/jit(_take)/gather | solution.py:35
  523.0 7.6 %gather_fusion.30 = f32[1024,2,16]{2,1,0:T(2,128)} fusion(f32[2,16,3072]{1,0,2:T(2,128)S(1)} %copy.179, s32[1024]{0:T(1024)} %fusion.111), kind=kCustom, calls=%fused_computation.30.clone | custom fusion | bytes 266240 | tf_op jit(solution)/shard_map/jit(_take)/gather | solution.py:35
  530.6 7.6 %gather_fusion.31 = f32[1024,2,16]{2,1,0:T(2,128)} fusion(f32[2,16,3072]{1,0,2:T(2,128)S(1)} %copy.179, s32[1024]{0:T(1024)} %fusion.112), kind=kCustom, calls=%fused_computation.31.clone | custom fusion | bytes 266240 | tf_op jit(solution)/shard_map/jit(_take)/gather | solution.py:35
  538.2 7.5 %gather_fusion.32 = f32[1024,2,16]{2,1,0:T(2,128)} fusion(f32[2,16,3072]{1,0,2:T(2,128)S(1)} %copy.179, s32[1024]{0:T(1024)S(1)} %copy-done.29), kind=kCustom, calls=%fused_computation.32.clone | custom fusion | bytes 266240 | tf_op jit(solution)/shard_map/jit(_take)/gather | solution.py:35
  545.7 7.5 %gather_fusion.33 = f32[1024,2,16]{2,1,0:T(2,128)} fusion(f32[2,16,3072]{1,0,2:T(2,128)S(1)} %copy.179, s32[1024]{0:T(1024)S(1)} %copy-done.28), kind=kCustom, calls=%fused_computation.33.clone | custom fusion | bytes 266240 | tf_op jit(solution)/shard_map/jit(_take)/gather | solution.py:35
  553.2 7.5 %gather_fusion.34 = f32[1024,2,16]{2,1,0:T(2,128)} fusion(f32[2,16,3072]{1,0,2:T(2,128)S(1)} %copy.179, s32[1024]{0:T(1024)S(1)} %fusion.115), kind=kCustom, calls=%fused_computation.34.clone | custom fusion | bytes 266240 | tf_op jit(solution)/shard_map/jit(_take)/gather | solution.py:35
  560.7 7.5 %gather_fusion.35 = f32[1024,2,16]{2,1,0:T(2,128)} fusion(f32[2,16,3072]{1,0,2:T(2,128)S(1)} %copy.179, s32[1024]{0:T(1024)S(1)} %fusion.116), kind=kCustom, calls=%fused_computation.35.clone | custom fusion | bytes 266240 | tf_op jit(solution)/shard_map/jit(_take)/gather | solution.py:35
  (194 shorter events, 118.8 us)
Async XLA Ops:
  0.7 27.7 %copy-start.35 = (pred[2048]{0:T(1024)(128)(4,1)}, pred[2048]{0:T(1024)(128)(4,1)S(1)}, u32[]{:S(2)}) copy-start(pred[2048]{0:T(1024)(128)(4,1)S(1)} %compare_and_fusion) | copy-start | bytes 6148
  16.5 17.1 %copy-start = (f32[2,16,1024]{2,1,0:T(8,128)S(1)}, f32[2,16,1024]{2,1,0:T(8,128)}, u32[]{:S(2)}) copy-start(f32[2,16,1024]{2,1,0:T(8,128)} %param.10) | copy-start | bytes 393220
  16.5 17.1 %copy-start.39 = (s32[8,1024]{1,0:T(8,128)S(1)}, s32[8,1024]{1,0:T(8,128)}, u32[]{:S(2)}) copy-start(s32[8,1024]{1,0:T(8,128)} %param.15) | copy-start | bytes 98308
  16.5 23.1 %copy-start.34 = (f32[2,8,1024]{2,1,0:T(8,128)S(1)}, f32[2,8,1024]{2,1,0:T(8,128)}, u32[]{:S(2)}) copy-start(f32[2,8,1024]{2,1,0:T(8,128)} %param.11) | copy-start | bytes 196612
  26.5 50.7 %copy-start.41 = (f32[1024]{0:T(1024)S(1)}, f32[1024]{0:T(1024)}, u32[]{:S(2)}) copy-start(f32[1024]{0:T(1024)} %param.13) | copy-start | bytes 12292
  26.6 51.9 %copy-start.40 = (f32[8,1024]{1,0:T(8,128)S(1)}, f32[8,1024]{1,0:T(8,128)}, u32[]{:S(2)}) copy-start(f32[8,1024]{1,0:T(8,128)} %param.12) | copy-start | bytes 98308
  28.5 50.6 %all-to-all-start = ((f32[2,16,8,256]{3,1,0,2:T(8,128)}), f32[2,16,8,256]{3,1,0,2:T(8,128)S(1)}, u32[]{:S(2)}, u32[]{:S(2)}) async-start(f32[2,16,8,256]{3,1,0,2:T(8,128)} %copy.120), calls=%async_computation | async-start | bytes 524288 | tf_op jit(solution)/shard_map/all_to_all | solution.py:30
  158.7 41.6 %copy-start.36 = (pred[2048]{0:T(1024)(128)(4,1)S(1)}, pred[2048]{0:T(1024)(128)(4,1)}, u32[]{:S(2)}) copy-start(pred[2048]{0:T(1024)(128)(4,1)} %copy-done.35) | copy-start | bytes 6148
  161.9 0.6 copy-start.11
  161.9 0.6 copy-start.13
  212.1 10.3 %all-to-all-start.1 = ((f32[2,16,8,256]{3,1,0,2:T(8,128)}), f32[2,16,8,256]{3,1,0,2:T(8,128)S(1)}, u32[]{:S(2)}, u32[]{:S(2)}) async-start(f32[2,16,8,256]{3,1,0,2:T(8,128)} %copy.139), calls=%async_computation.1 | async-start | bytes 524288 | tf_op jit(solution)/shard_map/all_to_all | solution.py:30
  287.9 10.4 %copy-start.9 = (f32[1024,2,16]{2,1,0:T(2,128)S(1)}, f32[1024,2,16]{2,1,0:T(2,128)}, u32[]{:S(2)}) copy-start(f32[1024,2,16]{2,1,0:T(2,128)} %gather_fusion.15) | copy-start | bytes 393220
  290.0 9.3 %copy-start.7 = (f32[1024,2,16]{2,1,0:T(2,128)S(1)}, f32[1024,2,16]{2,1,0:T(2,128)}, u32[]{:S(2)}) copy-start(f32[1024,2,16]{2,1,0:T(2,128)} %gather_fusion.16) | copy-start | bytes 393220
  292.2 7.6 %copy-start.5 = (f32[1024,2,16]{2,1,0:T(2,128)S(1)}, f32[1024,2,16]{2,1,0:T(2,128)}, u32[]{:S(2)}) copy-start(f32[1024,2,16]{2,1,0:T(2,128)} %gather_fusion.17) | copy-start | bytes 393220
  299.8 40.6 %copy-start.37 = (pred[2048]{0:T(1024)(128)(4,1)S(1)}, pred[2048]{0:T(1024)(128)(4,1)}, u32[]{:S(2)}) copy-start(pred[2048]{0:T(1024)(128)(4,1)} %copy-done.35) | copy-start | bytes 6148
  302.1 0.6 copy-start.15
  302.1 0.6 copy-start.17
  352.3 10.3 %all-to-all-start.2 = ((f32[2,16,8,256]{3,1,0,2:T(8,128)}), f32[2,16,8,256]{3,1,0,2:T(8,128)S(1)}, u32[]{:S(2)}, u32[]{:S(2)}) async-start(f32[2,16,8,256]{3,1,0,2:T(8,128)} %copy.158), calls=%async_computation.2 | async-start | bytes 524288 | tf_op jit(solution)/shard_map/all_to_all | solution.py:30
  428.1 10.4 %copy-start.10 = (f32[1024,2,16]{2,1,0:T(2,128)S(1)}, f32[1024,2,16]{2,1,0:T(2,128)}, u32[]{:S(2)}) copy-start(f32[1024,2,16]{2,1,0:T(2,128)} %gather_fusion.24) | copy-start | bytes 393220
  430.2 9.3 %copy-start.8 = (f32[1024,2,16]{2,1,0:T(2,128)S(1)}, f32[1024,2,16]{2,1,0:T(2,128)}, u32[]{:S(2)}) copy-start(f32[1024,2,16]{2,1,0:T(2,128)} %gather_fusion.25) | copy-start | bytes 393220
  432.4 7.6 %copy-start.6 = (f32[1024,2,16]{2,1,0:T(2,128)S(1)}, f32[1024,2,16]{2,1,0:T(2,128)}, u32[]{:S(2)}) copy-start(f32[1024,2,16]{2,1,0:T(2,128)} %gather_fusion.26) | copy-start | bytes 393220
  440.0 40.6 %copy-start.38 = (pred[2048]{0:T(1024)(128)(4,1)S(1)}, pred[2048]{0:T(1024)(128)(4,1)}, u32[]{:S(2)}) copy-start(pred[2048]{0:T(1024)(128)(4,1)} %copy-done.35) | copy-start | bytes 6148
  442.2 0.6 copy-start.19
  442.2 0.6 copy-start.21
  492.4 45.7 %copy-start.29 = (s32[1024]{0:T(1024)S(1)}, s32[1024]{0:T(1024)}, u32[]{:S(2)}) copy-start(s32[1024]{0:T(1024)} %fusion.113) | copy-start | bytes 12292
  492.4 10.4 %all-to-all-start.3 = ((f32[2,16,8,256]{3,1,0,2:T(8,128)}), f32[2,16,8,256]{3,1,0,2:T(8,128)S(1)}, u32[]{:S(2)}, u32[]{:S(2)}) async-start(f32[2,16,8,256]{3,1,0,2:T(8,128)} %copy.177), calls=%async_computation.3 | async-start | bytes 524288 | tf_op jit(solution)/shard_map/all_to_all | solution.py:30
  496.2 49.5 %copy-start.28 = (s32[1024]{0:T(1024)S(1)}, s32[1024]{0:T(1024)}, u32[]{:S(2)}) copy-start(s32[1024]{0:T(1024)} %fusion.114) | copy-start | bytes 12292
  568.2 6.2 %copy-start.1 = (f32[1024,2,16]{2,1,0:T(2,128)S(1)}, f32[1024,2,16]{2,1,0:T(2,128)}, u32[]{:S(2)}) copy-start(f32[1024,2,16]{2,1,0:T(2,128)} %gather_fusion.31) | copy-start | bytes 393220
  568.2 7.3 %copy-start.2 = (f32[1024,2,16]{2,1,0:T(2,128)S(1)}, f32[1024,2,16]{2,1,0:T(2,128)}, u32[]{:S(2)}) copy-start(f32[1024,2,16]{2,1,0:T(2,128)} %gather_fusion.32) | copy-start | bytes 393220
  568.2 8.4 %copy-start.3 = (f32[1024,2,16]{2,1,0:T(2,128)S(1)}, f32[1024,2,16]{2,1,0:T(2,128)}, u32[]{:S(2)}) copy-start(f32[1024,2,16]{2,1,0:T(2,128)} %gather_fusion.33) | copy-start | bytes 393220
  574.4 5.2 copy-start.30
  574.4 5.2 copy-start.31
  574.4 5.2 copy-start.32
  574.4 5.2 copy-start.33
  575.5 3.6 copy-start.4
  576.6 3.0 copy-start.20
  576.6 3.0 copy-start.22
  576.6 3.0 copy-start.23
  576.6 3.0 copy-start.24
  576.6 3.0 copy-start.25
  576.6 3.0 copy-start.26
  576.6 3.0 copy-start.27
  576.6 4.5 copy-start.12
  576.7 4.5 copy-start.14
  576.7 4.5 copy-start.16
  576.7 4.5 copy-start.18
where the time goes:
time: 585 us; the launch traced here: 582 us
  local copies, waits for them, and re-layouts  382 us (65%)
  blocking collectives  104 us (18%)
  other arithmetic  53 us (9%)
  waiting for transfers between devices  18.3 us (3%)
  starting transfers between devices  15.9 us (3%)
  matrix products  8.07 us (1%)
    gather x64, local copies, waits for them, and re-layouts, body(): jnp.take(extended, neighbours[apply_order], axis=2) - term  293 us
    psum x4, blocking collectives, body(): intersection = lax.psum(partial_intersection, 'mesh')  89.9 us
    gather x4, local copies, waits for them, and re-layouts, body(): jnp.take(term, routes.reshape(-1), axis=2).reshape(2, rows, parts, capacity)  57.7 us
    select_n x4, other arithmetic, body(): jnp.take(term, routes.reshape(-1), axis=2).reshape(2, rows, parts, capacity)  39.9 us
    all_to_all x4, waiting for transfers between devices, body(): lax.all_to_all(packed, 'mesh', split_axis=2, concat_axis=2, tiled=True)  18.3 us
    concatenate x4, local copies, waits for them, and re-layouts, body(): jnp.concatenate([term, arrived.reshape(2, rows, parts * capacity)], axis=2)  16.6 us
    all_to_all x4, starting transfers between devices, body(): lax.all_to_all(packed, 'mesh', split_axis=2, concat_axis=2, tiled=True)  15.9 us
    all_gather x1, blocking collectives, body(): full_frozen = lax.all_gather(frozen, 'band', axis=1, tiled=True)  14.2 us
  transfers between devices with their start and end apart: 4, of which 3 were waited for; matrix products, arithmetic and copies ran while one was open for 2% of the time, Pallas kernels for 0%

commit v1 on v0

--- a/solution.py
+++ b/solution.py
@@ -6,6 +6,18 @@
 NBRS = 8
 TERMS = 4
 time_step = 0.3
+
+
+def split_up(x, dim, size):
+    shape = x.shape
+    blocks = x.reshape(*shape[:dim], size, shape[dim] // size, *shape[dim + 1 :])
+    return jnp.moveaxis(blocks, dim, 0)
+
+
+def in_order(blocks, dim):
+    blocks = jnp.moveaxis(blocks, 0, dim)
+    shape = blocks.shape
+    return blocks.reshape(*shape[:dim], shape[dim] * shape[dim + 1], *shape[dim + 2 :])
 
 
 def rotate(field):
@@ -27,7 +39,14 @@
         )
         intersection = lax.psum(partial_intersection, "mesh")
         packed = jnp.take(term, routes.reshape(-1), axis=2).reshape(2, rows, parts, capacity)
-        arrived = lax.all_to_all(packed, "mesh", split_axis=2, concat_axis=2, tiled=True)
+        size, position = (lax.axis_size("mesh"), lax.axis_index("mesh"))
+        pieces = split_up(packed, 2, size)
+        done = [pieces[position]]
+        for step in range(1, size):
+            sent = pieces[position ^ step]
+            done.append(lax.ppermute(sent, "mesh", [(i, i ^ step) for i in range(size)]))
+        pieces = jnp.stack(done)[position ^ jnp.arange(size)]
+        arrived = in_order(pieces, 2)
         extended = jnp.concatenate([term, arrived.reshape(2, rows, parts * capacity)], axis=2)
         stencil = jnp.zeros_like(term)
         for apply_order in range(NBRS):

time: 585 us -> 557 us (0.952)
  local copies, waits for them, and re-layouts: 382 us -> 360 us
  other arithmetic: 53 us -> 41.7 us
  starting transfers between devices: 15.9 us -> 24.8 us
  waiting for transfers between devices: 18.3 us -> 11.7 us
    gather x4, local copies, waits for them, and re-layouts: 57.7 us -> 30.9 us  [body(): jnp.take(term, routes.reshape(-1), axis=2).reshape(2, rows, parts, capacity)]
    ppermute x0 -> x28, starting transfers between devices: none -> 24.8 us  [body(): lax.ppermute(sent, 'mesh', [(i, i ^ step) for i in range(size)])]
    all_to_all x4 -> x0, waiting for transfers between devices: 18.3 us -> none  [body(): lax.all_to_all(packed, 'mesh', split_axis=2, concat_axis=2, tiled=True)]
    all_to_all x4 -> x0, starting transfers between devices: 15.9 us -> none  [body(): lax.all_to_all(packed, 'mesh', split_axis=2, concat_axis=2, tiled=True)]
    ppermute x0 -> x28, waiting for transfers between devices: none -> 11.7 us  [body(): lax.ppermute(sent, 'mesh', [(i, i ^ step) for i in range(size)])]
    select_n x4, other arithmetic: 39.9 us -> 29.8 us  [body(): jnp.take(term, routes.reshape(-1), axis=2).reshape(2, rows, parts, capacity)]
    reshape x8 -> x0, local copies, waits for them, and re-layouts: 7.63 us -> none  [the longest x4 7.56 us: body(): jnp.take(term, routes.reshape(-1), axis=2).reshape(2, rows, parts, capacity)]
  transfers between devices with their start and end apart: 4 -> 28, of which waited for: 3 -> 7; matrix products, arithmetic and copies ran while one was open for 2% -> 2% of each run, Pallas kernels for 0% -> 0%
where the time goes in v1:
time: 557 us; the launch traced here: 555 us
  local copies, waits for them, and re-layouts  360 us (65%)
  blocking collectives  108 us (19%)
  other arithmetic  41.7 us (7%)
  starting transfers between devices  24.8 us (4%)
  waiting for transfers between devices  11.7 us (2%)
  matrix products  8.06 us (1%)
    gather x64, local copies, waits for them, and re-layouts, body(): jnp.take(extended, neighbours[apply_order], axis=2) - term  296 us
    psum x4, blocking collectives, body(): intersection = lax.psum(partial_intersection, 'mesh')  93.2 us
    gather x4, local copies, waits for them, and re-layouts, body(): jnp.take(term, routes.reshape(-1), axis=2).reshape(2, rows, parts, capacity)  30.9 us
    select_n x4, other arithmetic, body(): jnp.take(term, routes.reshape(-1), axis=2).reshape(2, rows, parts, capacity)  29.8 us
    ppermute x28, starting transfers between devices, body(): lax.ppermute(sent, 'mesh', [(i, i ^ step) for i in range(size)])  24.8 us
    concatenate x4, local copies, waits for them, and re-layouts, body(): jnp.concatenate([term, arrived.reshape(2, rows, parts * capacity)], axis=2)  16.6 us
    all_gather x1, blocking collectives, body(): full_frozen = lax.all_gather(frozen, 'band', axis=1, tiled=True)  14.4 us
    ppermute x28, waiting for transfers between devices, body(): lax.ppermute(sent, 'mesh', [(i, i ^ step) for i in range(size)])  11.7 us
  transfers between devices with their start and end apart: 28, of which 7 were waited for; matrix products, arithmetic and copies ran while one was open for 2% of the time, Pallas kernels for 0%

profile of v1, /device:TPU:0, one launch (start us, length us, event | category | flops | bytes accessed | tf_op | source)
XLA Modules:
  0.0 554.9 jit_solution(10426989873664411568)
XLA Ops:
  2.1 6.8 %gather_fusion.4 = f32[2048,2,16]{2,1,0:T(2,128)S(1)} fusion(f32[2,16,1024]{1,0,2:T(2,128)S(1)} %copy.131, s32[2048]{0:T(1024)S(1)} %fusion.108), kind=kCustom, calls=%fused_computation.clone | custom fusion | bytes 532480 | tf_op jit(solution)/shard_map/jit(_take)/gather | solution.py:41
  9.0 7.4 %broadcast_select_fusion.3 = f32[2048,2,16]{2,1,0:T(2,128)S(1)} fusion(f32[2048,2,16]{2,1,0:T(2,128)S(1)} %gather_fusion.4, pred[2048]{0:T(1024)(128)(4,1)S(1)} %compare_and_fusion), kind=kLoop, calls=%fused_computation.43 | loop fusion | flops 65536 | bytes 526336 | tf_op jit(solution)/shard_map/jit(_take)/select_n | solution.py:41
  27.1 14.4 %all_gather.3 = f32[2,32,1024]{2,1,0:T(8,128)S(1)} all-gather(f32[2,8,1024]{2,1,0:T(8,128)S(1)} %copy-done.32), channel_id=1, replica_groups=mesh['mesh'=8,'band'=4] {'band'}, dimensions={1}, use_global_device_ids=true | all-gather | bytes 327680 | tf_op jit(solution)/shard_map/all_gather | solution.py:32
  41.9 22.7 %psum.28 = f32[2,32,16]{1,2,0:T(8,128)S(1)} all-reduce(f32[2,32,16]{1,2,0:T(8,128)S(1)} %convolution_bitcast_fusion.7), channel_id=1, replica_groups=mesh['mesh'=8,'band'=4] {'mesh'}, use_global_device_ids=true, to_apply=%region_0.3 | all-reduce | flops 1024 | bytes 8192 | tf_op jit(solution)/shard_map/psum | solution.py:40
  66.9 4.6 collective-permute-done.5
  73.1 4.1 copy.141
  77.3 7.7 %gather_fusion.5 = f32[1024,2,16]{2,1,0:T(2,128)} fusion(f32[2,16,3072]{1,0,2:T(2,128)S(1)} %copy.141, s32[1024]{0:T(1024)} %get-tuple-element.100), kind=kCustom, calls=%fused_computation.1.clone | custom fusion | bytes 266240 | tf_op jit(solution)/shard_map/jit(_take)/gather | solution.py:54
  87.0 7.7 %gather_fusion.6 = f32[1024,2,16]{2,1,0:T(2,128)} fusion(f32[2,16,3072]{1,0,2:T(2,128)S(1)} %copy.141, s32[1024]{0:T(1024)} %get-tuple-element.101), kind=kCustom, calls=%fused_computation.5.clone | custom fusion | bytes 266240 | tf_op jit(solution)/shard_map/jit(_take)/gather | solution.py:54
  96.6 7.7 %gather_fusion.7 = f32[1024,2,16]{2,1,0:T(2,128)} fusion(f32[2,16,3072]{1,0,2:T(2,128)S(1)} %copy.141, s32[1024]{0:T(1024)} %get-tuple-element.102), kind=kCustom, calls=%fused_computation.6.clone | custom fusion | bytes 266240 | tf_op jit(solution)/shard_map/jit(_take)/gather | solution.py:54
  106.3 7.7 %gather_fusion.8 = f32[1024,2,16]{2,1,0:T(2,128)} fusion(f32[2,16,3072]{1,0,2:T(2,128)S(1)} %copy.141, s32[1024]{0:T(1024)} %get-tuple-element.103), kind=kCustom, calls=%fused_computation.7.clone | custom fusion | bytes 266240 | tf_op jit(solution)/shard_map/jit(_take)/gather | solution.py:54
  116.0 7.7 %gather_fusion.9 = f32[1024,2,16]{2,1,0:T(2,128)} fusion(f32[2,16,3072]{1,0,2:T(2,128)S(1)} %copy.141, s32[1024]{0:T(1024)} %get-tuple-element.104), kind=kCustom, calls=%fused_computation.8.clone | custom fusion | bytes 266240 | tf_op jit(solution)/shard_map/jit(_take)/gather | solution.py:54
  125.7 7.7 %gather_fusion.10 = f32[1024,2,16]{2,1,0:T(2,128)} fusion(f32[2,16,3072]{1,0,2:T(2,128)S(1)} %copy.141, s32[1024]{0:T(1024)} %get-tuple-element.105), kind=kCustom, calls=%fused_computation.9.clone | custom fusion | bytes 266240 | tf_op jit(solution)/shard_map/jit(_take)/gather | solution.py:54
  135.4 7.7 %gather_fusion.11 = f32[1024,2,16]{2,1,0:T(2,128)} fusion(f32[2,16,3072]{1,0,2:T(2,128)S(1)} %copy.141, s32[1024]{0:T(1024)} %get-tuple-element.106), kind=kCustom, calls=%fused_computation.10.clone | custom fusion | bytes 266240 | tf_op jit(solution)/shard_map/jit(_take)/gather | solution.py:54
  145.0 7.7 %gather_fusion.12 = f32[1024,2,16]{2,1,0:T(2,128)} fusion(f32[2,16,3072]{1,0,2:T(2,128)S(1)} %copy.141, s32[1024]{0:T(1024)} %get-tuple-element.107), kind=kCustom, calls=%fused_computation.11.clone | custom fusion | bytes 266240 | tf_op jit(solution)/shard_map/jit(_take)/gather | solution.py:54
  158.2 22.5 %psum.29 = f32[2,32,16]{1,2,0:T(8,128)S(1)} all-reduce(f32[2,32,16]{1,2,0:T(8,128)S(1)} %convolution_bitcast_fusion.6), channel_id=1, replica_groups=mesh['mesh'=8,'band'=4] {'mesh'}, use_global_device_ids=true, to_apply=%region_1.4 | all-reduce | flops 1024 | bytes 8192 | tf_op jit(solution)/shard_map/psum | solution.py:40
  180.7 8.0 %gather_fusion.13 = f32[2048,2,16]{2,1,0:T(2,128)S(1)} fusion(f32[2,16,1024]{1,0,2:T(2,128)} %copy.157, s32[2048]{0:T(1024)S(1)} %fusion.108), kind=kCustom, calls=%fused_computation.2.clone | custom fusion | bytes 532480 | tf_op jit(solution)/shard_map/jit(_take)/gather | solution.py:41
  188.8 7.4 %broadcast_select_fusion.2 = f32[2048,2,16]{2,1,0:T(2,128)S(1)} fusion(f32[2048,2,16]{2,1,0:T(2,128)S(1)} %gather_fusion.13, pred[2048]{0:T(1024)(128)(4,1)S(1)} %copy-done.34), kind=kLoop, calls=%fused_computation.42 | loop fusion | flops 65536 | bytes 526336 | tf_op jit(solution)/shard_map/jit(_take)/select_n | solution.py:41
  212.7 7.7 %gather_fusion.14 = f32[1024,2,16]{2,1,0:T(2,128)} fusion(f32[2,16,3072]{1,0,2:T(2,128)S(1)} %copy.167, s32[1024]{0:T(1024)} %get-tuple-element.100), kind=kCustom, calls=%fused_computation.12.clone | custom fusion | bytes 266240 | tf_op jit(solution)/shard_map/jit(_take)/gather | solution.py:54
  220.3 7.7 %gather_fusion.15 = f32[1024,2,16]{2,1,0:T(2,128)} fusion(f32[2,16,3072]{1,0,2:T(2,128)S(1)} %copy.167, s32[1024]{0:T(1024)} %get-tuple-element.101), kind=kCustom, calls=%fused_computation.13.clone | custom fusion | bytes 266240 | tf_op jit(solution)/shard_map/jit(_take)/gather | solution.py:54
  228.0 7.7 %gather_fusion.16 = f32[1024,2,16]{2,1,0:T(2,128)} fusion(f32[2,16,3072]{1,0,2:T(2,128)S(1)} %copy.167, s32[1024]{0:T(1024)} %get-tuple-element.102), kind=kCustom, calls=%fused_computation.14.clone | custom fusion | bytes 266240 | tf_op jit(solution)/shard_map/jit(_take)/gather | solution.py:54
  235.7 7.7 %gather_fusion.17 = f32[1024,2,16]{2,1,0:T(2,128)} fusion(f32[2,16,3072]{1,0,2:T(2,128)S(1)} %copy.167, s32[1024]{0:T(1024)} %get-tuple-element.103), kind=kCustom, calls=%fused_computation.15.clone | custom fusion | bytes 266240 | tf_op jit(solution)/shard_map/jit(_take)/gather | solution.py:54
  243.3 7.7 %gather_fusion.18 = f32[1024,2,16]{2,1,0:T(2,128)} fusion(f32[2,16,3072]{1,0,2:T(2,128)S(1)} %copy.167, s32[1024]{0:T(1024)} %get-tuple-element.104), kind=kCustom, calls=%fused_computation.16.clone | custom fusion | bytes 266240 | tf_op jit(solution)/shard_map/jit(_take)/gather | solution.py:54
  251.0 7.6 %gather_fusion.19 = f32[1024,2,16]{2,1,0:T(2,128)} fusion(f32[2,16,3072]{1,0,2:T(2,128)S(1)} %copy.167, s32[1024]{0:T(1024)} %get-tuple-element.105), kind=kCustom, calls=%fused_computation.17.clone | custom fusion | bytes 266240 | tf_op jit(solution)/shard_map/jit(_take)/gather | solution.py:54
  258.7 7.6 %gather_fusion.20 = f32[1024,2,16]{2,1,0:T(2,128)} fusion(f32[2,16,3072]{1,0,2:T(2,128)S(1)} %copy.167, s32[1024]{0:T(1024)} %get-tuple-element.106), kind=kCustom, calls=%fused_computation.18.clone | custom fusion | bytes 266240 | tf_op jit(solution)/shard_map/jit(_take)/gather | solution.py:54
  266.3 7.7 %gather_fusion.21 = f32[1024,2,16]{2,1,0:T(2,128)} fusion(f32[2,16,3072]{1,0,2:T(2,128)S(1)} %copy.167, s32[1024]{0:T(1024)} %get-tuple-element.107), kind=kCustom, calls=%fused_computation.19.clone | custom fusion | bytes 266240 | tf_op jit(solution)/shard_map/jit(_take)/gather | solution.py:54
  290.4 24.0 %psum.30 = f32[2,32,16]{1,2,0:T(8,128)S(1)} all-reduce(f32[2,32,16]{1,2,0:T(8,128)S(1)} %convolution_bitcast_fusion.5), channel_id=1, replica_groups=mesh['mesh'=8,'band'=4] {'mesh'}, use_global_device_ids=true, to_apply=%region_2.5 | all-reduce | flops 1024 | bytes 8192 | tf_op jit(solution)/shard_map/psum | solution.py:40
  314.4 8.0 %gather_fusion.22 = f32[2048,2,16]{2,1,0:T(2,128)S(1)} fusion(f32[2,16,1024]{1,0,2:T(2,128)} %copy.183, s32[2048]{0:T(1024)S(1)} %fusion.108), kind=kCustom, calls=%fused_computation.3.clone | custom fusion | bytes 532480 | tf_op jit(solution)/shard_map/jit(_take)/gather | solution.py:41
  322.5 7.4 %broadcast_select_fusion.1 = f32[2048,2,16]{2,1,0:T(2,128)S(1)} fusion(f32[2048,2,16]{2,1,0:T(2,128)S(1)} %gather_fusion.22, pred[2048]{0:T(1024)(128)(4,1)S(1)} %copy-done.35), kind=kLoop, calls=%fused_computation.41 | loop fusion | flops 65536 | bytes 526336 | tf_op jit(solution)/shard_map/jit(_take)/select_n | solution.py:41
  346.4 7.7 %gather_fusion.23 = f32[1024,2,16]{2,1,0:T(2,128)} fusion(f32[2,16,3072]{1,0,2:T(2,128)S(1)} %copy.193, s32[1024]{0:T(1024)} %get-tuple-element.100), kind=kCustom, calls=%fused_computation.20.clone | custom fusion | bytes 266240 | tf_op jit(solution)/shard_map/jit(_take)/gather | solution.py:54
  354.1 7.7 %gather_fusion.24 = f32[1024,2,16]{2,1,0:T(2,128)} fusion(f32[2,16,3072]{1,0,2:T(2,128)S(1)} %copy.193, s32[1024]{0:T(1024)} %get-tuple-element.101), kind=kCustom, calls=%fused_computation.21.clone | custom fusion | bytes 266240 | tf_op jit(solution)/shard_map/jit(_take)/gather | solution.py:54
  361.8 7.7 %gather_fusion.25 = f32[1024,2,16]{2,1,0:T(2,128)} fusion(f32[2,16,3072]{1,0,2:T(2,128)S(1)} %copy.193, s32[1024]{0:T(1024)} %get-tuple-element.102), kind=kCustom, calls=%fused_computation.22.clone | custom fusion | bytes 266240 | tf_op jit(solution)/shard_map/jit(_take)/gather | solution.py:54
  369.4 7.7 %gather_fusion.26 = f32[1024,2,16]{2,1,0:T(2,128)} fusion(f32[2,16,3072]{1,0,2:T(2,128)S(1)} %copy.193, s32[1024]{0:T(1024)} %get-tuple-element.103), kind=kCustom, calls=%fused_computation.23.clone | custom fusion | bytes 266240 | tf_op jit(solution)/shard_map/jit(_take)/gather | solution.py:54
  377.1 7.7 %gather_fusion.27 = f32[1024,2,16]{2,1,0:T(2,128)} fusion(f32[2,16,3072]{1,0,2:T(2,128)S(1)} %copy.193, s32[1024]{0:T(1024)} %get-tuple-element.104), kind=kCustom, calls=%fused_computation.24.clone | custom fusion | bytes 266240 | tf_op jit(solution)/shard_map/jit(_take)/gather | solution.py:54
  384.8 7.6 %gather_fusion.28 = f32[1024,2,16]{2,1,0:T(2,128)} fusion(f32[2,16,3072]{1,0,2:T(2,128)S(1)} %copy.193, s32[1024]{0:T(1024)} %get-tuple-element.105), kind=kCustom, calls=%fused_computation.25.clone | custom fusion | bytes 266240 | tf_op jit(solution)/shard_map/jit(_take)/gather | solution.py:54
  392.4 7.6 %gather_fusion.29 = f32[1024,2,16]{2,1,0:T(2,128)} fusion(f32[2,16,3072]{1,0,2:T(2,128)S(1)} %copy.193, s32[1024]{0:T(1024)} %get-tuple-element.106), kind=kCustom, calls=%fused_computation.26.clone | custom fusion | bytes 266240 | tf_op jit(solution)/shard_map/jit(_take)/gather | solution.py:54
  400.1 7.7 %gather_fusion.30 = f32[1024,2,16]{2,1,0:T(2,128)} fusion(f32[2,16,3072]{1,0,2:T(2,128)S(1)} %copy.193, s32[1024]{0:T(1024)} %get-tuple-element.107), kind=kCustom, calls=%fused_computation.27.clone | custom fusion | bytes 266240 | tf_op jit(solution)/shard_map/jit(_take)/gather | solution.py:54
  424.2 24.0 %psum.31 = f32[2,32,16]{1,2,0:T(8,128)S(1)} all-reduce(f32[2,32,16]{1,2,0:T(8,128)S(1)} %convolution_bitcast_fusion.4), channel_id=1, replica_groups=mesh['mesh'=8,'band'=4] {'mesh'}, use_global_device_ids=true, to_apply=%region_3.6 | all-reduce | flops 1024 | bytes 8192 | tf_op jit(solution)/shard_map/psum | solution.py:40
  448.2 8.0 %gather_fusion.31 = f32[2048,2,16]{2,1,0:T(2,128)S(1)} fusion(f32[2,16,1024]{1,0,2:T(2,128)} %copy.209, s32[2048]{0:T(1024)S(1)} %fusion.108), kind=kCustom, calls=%fused_computation.4.clone | custom fusion | bytes 532480 | tf_op jit(solution)/shard_map/jit(_take)/gather | solution.py:41
  456.2 7.4 %broadcast_select_fusion = f32[2048,2,16]{2,1,0:T(2,128)S(1)} fusion(f32[2048,2,16]{2,1,0:T(2,128)S(1)} %gather_fusion.31, pred[2048]{0:T(1024)(128)(4,1)S(1)} %copy-done.36), kind=kLoop, calls=%fused_computation.40 | loop fusion | flops 65536 | bytes 526336 | tf_op jit(solution)/shard_map/jit(_take)/select_n | solution.py:41
  476.0 4.1 copy.219
  480.2 7.6 %gather_fusion.32 = f32[1024,2,16]{2,1,0:T(2,128)} fusion(f32[2,16,3072]{1,0,2:T(2,128)S(1)} %copy.219, s32[1024]{0:T(1024)} %get-tuple-element.100), kind=kCustom, calls=%fused_computation.28.clone | custom fusion | bytes 266240 | tf_op jit(solution)/shard_map/jit(_take)/gather | solution.py:54
  487.8 7.6 %gather_fusion.33 = f32[1024,2,16]{2,1,0:T(2,128)} fusion(f32[2,16,3072]{1,0,2:T(2,128)S(1)} %copy.219, s32[1024]{0:T(1024)} %get-tuple-element.101), kind=kCustom, calls=%fused_computation.29.clone | custom fusion | bytes 266240 | tf_op jit(solution)/shard_map/jit(_take)/gather | solution.py:54
  495.4 7.7 %gather_fusion.34 = f32[1024,2,16]{2,1,0:T(2,128)} fusion(f32[2,16,3072]{1,0,2:T(2,128)S(1)} %copy.219, s32[1024]{0:T(1024)} %get-tuple-element.102), kind=kCustom, calls=%fused_computation.30.clone | custom fusion | bytes 266240 | tf_op jit(solution)/shard_map/jit(_take)/gather | solution.py:54
  503.1 7.7 %gather_fusion.35 = f32[1024,2,16]{2,1,0:T(2,128)} fusion(f32[2,16,3072]{1,0,2:T(2,128)S(1)} %copy.219, s32[1024]{0:T(1024)} %get-tuple-element.103), kind=kCustom, calls=%fused_computation.31.clone | custom fusion | bytes 266240 | tf_op jit(solution)/shard_map/jit(_take)/gather | solution.py:54
  510.8 7.6 %gather_fusion.36 = f32[1024,2,16]{2,1,0:T(2,128)} fusion(f32[2,16,3072]{1,0,2:T(2,128)S(1)} %copy.219, s32[1024]{0:T(1024)} %get-tuple-element.104), kind=kCustom, calls=%fused_computation.32.clone | custom fusion | bytes 266240 | tf_op jit(solution)/shard_map/jit(_take)/gather | solution.py:54
  518.4 7.7 %gather_fusion.37 = f32[1024,2,16]{2,1,0:T(2,128)} fusion(f32[2,16,3072]{1,0,2:T(2,128)S(1)} %copy.219, s32[1024]{0:T(1024)} %get-tuple-element.105), kind=kCustom, calls=%fused_computation.33.clone | custom fusion | bytes 266240 | tf_op jit(solution)/shard_map/jit(_take)/gather | solution.py:54
  526.1 7.6 %gather_fusion.38 = f32[1024,2,16]{2,1,0:T(2,128)} fusion(f32[2,16,3072]{1,0,2:T(2,128)S(1)} %copy.219, s32[1024]{0:T(1024)S(1)} %copy-done.31), kind=kCustom, calls=%fused_computation.34.clone | custom fusion | bytes 266240 | tf_op jit(solution)/shard_map/jit(_take)/gather | solution.py:54
  533.7 7.5 %gather_fusion.39 = f32[1024,2,16]{2,1,0:T(2,128)} fusion(f32[2,16,3072]{1,0,2:T(2,128)S(1)} %copy.219, s32[1024]{0:T(1024)S(1)} %copy-done.30), kind=kCustom, calls=%fused_computation.35.clone | custom fusion | bytes 266240 | tf_op jit(solution)/shard_map/jit(_take)/gather | solution.py:54
  (310 shorter events, 127.5 us)
Async XLA Ops:
  0.7 8.2 %copy-start.33 = (pred[2048]{0:T(1024)(128)(4,1)}, pred[2048]{0:T(1024)(128)(4,1)S(1)}, u32[]{:S(2)}) copy-start(pred[2048]{0:T(1024)(128)(4,1)S(1)} %compare_and_fusion) | copy-start | bytes 6148
  16.4 5.9 %copy-start.37 = (s32[8,1024]{1,0:T(8,128)S(1)}, s32[8,1024]{1,0:T(8,128)}, u32[]{:S(2)}) copy-start(s32[8,1024]{1,0:T(8,128)} %param.15) | copy-start | bytes 98308
  16.4 10.7 %copy-start.32 = (f32[2,8,1024]{2,1,0:T(8,128)S(1)}, f32[2,8,1024]{2,1,0:T(8,128)}, u32[]{:S(2)}) copy-start(f32[2,8,1024]{2,1,0:T(8,128)} %param.11) | copy-start | bytes 196612
  16.5 48.1 %copy-start.38 = (f32[8,1024]{1,0:T(8,128)S(1)}, f32[8,1024]{1,0:T(8,128)}, u32[]{:S(2)}) copy-start(f32[8,1024]{1,0:T(8,128)} %param.12) | copy-start | bytes 98308
  16.5 48.7 %copy-start.39 = (f32[1024]{0:T(1024)S(1)}, f32[1024]{0:T(1024)}, u32[]{:S(2)}) copy-start(f32[1024]{0:T(1024)} %param.13) | copy-start | bytes 12292
  16.8 49.9 %collective-permute-start = (f32[2,16,1,256]{3,1,0,2:T(8,128)S(1)}, f32[2,16,1,256]{3,1,0,2:T(8,128)S(1)}, u32[]{:S(2)}, u32[]{:S(2)}) collective-permute-start(f32[2,16,1,256]{3,1,0,2:T(8,128)S(1)} %bitcast.581), channel_id=1, source_target_pairs={{0,4},{4,0},{8,12},{12,8},{16,20},{20,16},{24,28},{28,24},{1,5},{5... | collective-permute-start | bytes 98312 | tf_op jit(solution)/shard_map/ppermute | solution.py:47
  17.4 49.4 %collective-permute-start.1 = (f32[2,16,1,256]{3,1,0,2:T(8,128)S(1)}, f32[2,16,1,256]{3,1,0,2:T(8,128)S(1)}, u32[]{:S(2)}, u32[]{:S(2)}) collective-permute-start(f32[2,16,1,256]{3,1,0,2:T(8,128)S(1)} %bitcast.580), channel_id=1, source_target_pairs={{0,8},{4,12},{8,0},{12,4},{16,24},{20,28},{24,16},{28,20},{1,9},{5... | collective-permute-start | bytes 98312 | tf_op jit(solution)/shard_map/ppermute | solution.py:47
  20.0 46.8 %collective-permute-start.2 = (f32[2,16,1,256]{3,1,0,2:T(8,128)S(1)}, f32[2,16,1,256]{3,1,0,2:T(8,128)S(1)}, u32[]{:S(2)}, u32[]{:S(2)}) collective-permute-start(f32[2,16,1,256]{3,1,0,2:T(8,128)S(1)} %bitcast.579), channel_id=1, source_target_pairs={{0,12},{4,8},{8,4},{12,0},{16,28},{20,24},{24,20},{28,16},{1,13},{... | collective-permute-start | bytes 98312 | tf_op jit(solution)/shard_map/ppermute | solution.py:47
  20.3 46.6 %collective-permute-start.3 = (f32[2,16,1,256]{3,1,0,2:T(8,128)S(1)}, f32[2,16,1,256]{3,1,0,2:T(8,128)S(1)}, u32[]{:S(2)}, u32[]{:S(2)}) collective-permute-start(f32[2,16,1,256]{3,1,0,2:T(8,128)S(1)} %bitcast.578), channel_id=1, source_target_pairs={{0,16},{4,20},{8,24},{12,28},{16,0},{20,4},{24,8},{28,12},{1,17},{... | collective-permute-start | bytes 98312 | tf_op jit(solution)/shard_map/ppermute | solution.py:47
  22.2 44.7 %collective-permute-start.4 = (f32[2,16,1,256]{3,1,0,2:T(8,128)S(1)}, f32[2,16,1,256]{3,1,0,2:T(8,128)S(1)}, u32[]{:S(2)}, u32[]{:S(2)}) collective-permute-start(f32[2,16,1,256]{3,1,0,2:T(8,128)S(1)} %bitcast.577), channel_id=1, source_target_pairs={{0,20},{4,16},{8,28},{12,24},{16,4},{20,0},{24,12},{28,8},{1,21},{... | collective-permute-start | bytes 98312 | tf_op jit(solution)/shard_map/ppermute | solution.py:47
  66.4 5.9 %copy-start.40 = (s32[1024]{0:T(1024)}, s32[1024]{0:T(1024)S(1)}, u32[]{:S(2)}) copy-start(s32[1024]{0:T(1024)S(1)} %pad_clamp_fusion) | copy-start | bytes 12292
  66.6 4.9 collective-permute-start.5
  66.7 4.8 collective-permute-start.6
  152.7 36.1 %copy-start.34 = (pred[2048]{0:T(1024)(128)(4,1)S(1)}, pred[2048]{0:T(1024)(128)(4,1)}, u32[]{:S(2)}) copy-start(pred[2048]{0:T(1024)(128)(4,1)} %copy-done.33) | copy-start | bytes 6148
  196.6 5.0 collective-permute-start.7
  196.8 5.6 %collective-permute-start.8 = (f32[2,16,1,256]{3,1,0,2:T(8,128)S(1)}, f32[2,16,1,256]{3,1,0,2:T(8,128)S(1)}, u32[]{:S(2)}, u32[]{:S(2)}) collective-permute-start(f32[2,16,1,256]{3,1,0,2:T(8,128)S(1)} %bitcast.599), channel_id=1, source_target_pairs={{0,8},{4,12},{8,0},{12,4},{16,24},{20,28},{24,16},{28,20},{1,9},{5... | collective-permute-start | bytes 98312 | tf_op jit(solution)/shard_map/ppermute | solution.py:47
  197.0 7.5 %collective-permute-start.9 = (f32[2,16,1,256]{3,1,0,2:T(8,128)S(1)}, f32[2,16,1,256]{3,1,0,2:T(8,128)S(1)}, u32[]{:S(2)}, u32[]{:S(2)}) collective-permute-start(f32[2,16,1,256]{3,1,0,2:T(8,128)S(1)} %bitcast.589), channel_id=1, source_target_pairs={{0,12},{4,8},{8,4},{12,0},{16,28},{20,24},{24,20},{28,16},{1,13},{... | collective-permute-start | bytes 98312 | tf_op jit(solution)/shard_map/ppermute | solution.py:47
  198.9 5.5 collective-permute-start.10
  200.3 4.2 collective-permute-start.11
  201.6 5.0 collective-permute-start.12
  202.4 4.4 collective-permute-start.13
  274.0 10.4 %copy-start.9 = (f32[1024,2,16]{2,1,0:T(2,128)S(1)}, f32[1024,2,16]{2,1,0:T(2,128)}, u32[]{:S(2)}) copy-start(f32[1024,2,16]{2,1,0:T(2,128)} %gather_fusion.19) | copy-start | bytes 393220
  276.1 9.3 %copy-start.7 = (f32[1024,2,16]{2,1,0:T(2,128)S(1)}, f32[1024,2,16]{2,1,0:T(2,128)}, u32[]{:S(2)}) copy-start(f32[1024,2,16]{2,1,0:T(2,128)} %gather_fusion.20) | copy-start | bytes 393220
  278.2 7.6 %copy-start.5 = (f32[1024,2,16]{2,1,0:T(2,128)S(1)}, f32[1024,2,16]{2,1,0:T(2,128)}, u32[]{:S(2)}) copy-start(f32[1024,2,16]{2,1,0:T(2,128)} %gather_fusion.21) | copy-start | bytes 393220
  285.9 36.6 %copy-start.35 = (pred[2048]{0:T(1024)(128)(4,1)S(1)}, pred[2048]{0:T(1024)(128)(4,1)}, u32[]{:S(2)}) copy-start(pred[2048]{0:T(1024)(128)(4,1)} %copy-done.33) | copy-start | bytes 6148
  330.3 5.0 collective-permute-start.14
  330.5 5.6 %collective-permute-start.15 = (f32[2,16,1,256]{3,1,0,2:T(8,128)S(1)}, f32[2,16,1,256]{3,1,0,2:T(8,128)S(1)}, u32[]{:S(2)}, u32[]{:S(2)}) collective-permute-start(f32[2,16,1,256]{3,1,0,2:T(8,128)S(1)} %bitcast.600), channel_id=1, source_target_pairs={{0,8},{4,12},{8,0},{12,4},{16,24},{20,28},{24,16},{28,20},{1,9},{5... | collective-permute-start | bytes 98312 | tf_op jit(solution)/shard_map/ppermute | solution.py:47
  330.7 7.5 %collective-permute-start.16 = (f32[2,16,1,256]{3,1,0,2:T(8,128)S(1)}, f32[2,16,1,256]{3,1,0,2:T(8,128)S(1)}, u32[]{:S(2)}, u32[]{:S(2)}) collective-permute-start(f32[2,16,1,256]{3,1,0,2:T(8,128)S(1)} %bitcast.591), channel_id=1, source_target_pairs={{0,12},{4,8},{8,4},{12,0},{16,28},{20,24},{24,20},{28,16},{1,13},{... | collective-permute-start | bytes 98312 | tf_op jit(solution)/shard_map/ppermute | solution.py:47
  332.7 5.5 collective-permute-start.17
  334.0 4.2 collective-permute-start.18
  335.3 5.0 collective-permute-start.19
  336.2 4.4 collective-permute-start.20
  407.7 10.4 %copy-start.10 = (f32[1024,2,16]{2,1,0:T(2,128)S(1)}, f32[1024,2,16]{2,1,0:T(2,128)}, u32[]{:S(2)}) copy-start(f32[1024,2,16]{2,1,0:T(2,128)} %gather_fusion.28) | copy-start | bytes 393220
  409.8 9.3 %copy-start.8 = (f32[1024,2,16]{2,1,0:T(2,128)S(1)}, f32[1024,2,16]{2,1,0:T(2,128)}, u32[]{:S(2)}) copy-start(f32[1024,2,16]{2,1,0:T(2,128)} %gather_fusion.29) | copy-start | bytes 393220
  411.9 7.6 %copy-start.6 = (f32[1024,2,16]{2,1,0:T(2,128)S(1)}, f32[1024,2,16]{2,1,0:T(2,128)}, u32[]{:S(2)}) copy-start(f32[1024,2,16]{2,1,0:T(2,128)} %gather_fusion.30) | copy-start | bytes 393220
  419.6 36.6 %copy-start.36 = (pred[2048]{0:T(1024)(128)(4,1)S(1)}, pred[2048]{0:T(1024)(128)(4,1)}, u32[]{:S(2)}) copy-start(pred[2048]{0:T(1024)(128)(4,1)} %copy-done.33) | copy-start | bytes 6148
  464.1 5.0 collective-permute-start.21
  464.2 5.6 %collective-permute-start.22 = (f32[2,16,1,256]{3,1,0,2:T(8,128)S(1)}, f32[2,16,1,256]{3,1,0,2:T(8,128)S(1)}, u32[]{:S(2)}, u32[]{:S(2)}) collective-permute-start(f32[2,16,1,256]{3,1,0,2:T(8,128)S(1)} %bitcast.601), channel_id=1, source_target_pairs={{0,8},{4,12},{8,0},{12,4},{16,24},{20,28},{24,16},{28,20},{1,9},{5... | collective-permute-start | bytes 98312 | tf_op jit(solution)/shard_map/ppermute | solution.py:47
  464.4 7.5 %collective-permute-start.23 = (f32[2,16,1,256]{3,1,0,2:T(8,128)S(1)}, f32[2,16,1,256]{3,1,0,2:T(8,128)S(1)}, u32[]{:S(2)}, u32[]{:S(2)}) collective-permute-start(f32[2,16,1,256]{3,1,0,2:T(8,128)S(1)} %bitcast.593), channel_id=1, source_target_pairs={{0,12},{4,8},{8,4},{12,0},{16,28},{20,24},{24,20},{28,16},{1,13},{... | collective-permute-start | bytes 98312 | tf_op jit(solution)/shard_map/ppermute | solution.py:47
  466.4 5.5 collective-permute-start.24
  467.7 4.2 collective-permute-start.25
  469.1 5.0 collective-permute-start.26
  469.9 4.4 collective-permute-start.27
  475.2 51.0 %copy-start.31 = (s32[1024]{0:T(1024)S(1)}, s32[1024]{0:T(1024)}, u32[]{:S(2)}) copy-start(s32[1024]{0:T(1024)} %get-tuple-element.106) | copy-start | bytes 12292
  475.2 58.5 %copy-start.30 = (s32[1024]{0:T(1024)S(1)}, s32[1024]{0:T(1024)}, u32[]{:S(2)}) copy-start(s32[1024]{0:T(1024)} %get-tuple-element.107) | copy-start | bytes 12292
  541.2 6.2 %copy-start.1 = (f32[1024,2,16]{2,1,0:T(2,128)S(1)}, f32[1024,2,16]{2,1,0:T(2,128)}, u32[]{:S(2)}) copy-start(f32[1024,2,16]{2,1,0:T(2,128)} %gather_fusion.35) | copy-start | bytes 393220
  541.2 7.3 %copy-start.2 = (f32[1024,2,16]{2,1,0:T(2,128)S(1)}, f32[1024,2,16]{2,1,0:T(2,128)}, u32[]{:S(2)}) copy-start(f32[1024,2,16]{2,1,0:T(2,128)} %gather_fusion.36) | copy-start | bytes 393220
  541.2 8.4 %copy-start.3 = (f32[1024,2,16]{2,1,0:T(2,128)S(1)}, f32[1024,2,16]{2,1,0:T(2,128)}, u32[]{:S(2)}) copy-start(f32[1024,2,16]{2,1,0:T(2,128)} %gather_fusion.37) | copy-start | bytes 393220
  (21 other events, 62.6 us)
